TPU v7x, 32 devices: a whole 2x2x4 slice. The times are simulated.
32 devices in a mesh: row: 4 (over y, x), col: 8 (over z, core).
Axes of the slice: x: 2, y: 2, z: 4, core: 2. Of those that a mesh axis runs over, the one named last changes fastest.
Arguments:
- eigvecs: float32 [4096, 4096], P('row', 'col'), may hold values from -6 to 6
- house_one: float32 [4096, 128], P('row', 'col'), may hold values from -0.09375 to 0.09375
- house_two: float32 [4096, 128], P('row', 'col'), may hold values from -0.09375 to 0.09375
- tile_map: int32 [32], replicated, may hold values from 0 to 31, each once
- select: int32 [256], replicated, may hold values from 0 to 4095, as said below
- ritz_basis: bfloat16 [32768, 4096], P(('row', 'col')), may hold values from -0.09375 to 0.09375
Outputs:
- back_vectors: float32 [4096, 4096], P('row', 'col')
- mode_shapes: bfloat16 [32768, 256], P(('row', 'col'))
Inputs may be any that keep to these rules, and one draw needn't show every extreme that they name: `select`: the 256 indices are distinct and include 0 and 4095. `tile_map`: each global tile row appears once.
All inputs are finite; a program needn't handle non-finite values.
Results may differ from a plain program's by a relative error of at most 0.0049.
Values may be sent and summed in bfloat16 or wider, within the bound.
No kernel may reach another device: no remote copies, remote signals or barrier semaphores. Data moves between devices by JAX's collectives and lax.ppermute only.
A program may use at most 64 MiB of HBM per device.

v0:
```python
import jax
import jax.numpy as jnp
from jax import lax
from jax.sharding import PartitionSpec as P

TILE = 128


def precise(left, right):
    return jnp.dot(left, right, precision=lax.Precision.HIGHEST, preferred_element_type=jnp.float32)


def compact(gram):
    width = gram.shape[0]
    scales = 0.5 * jnp.diag(gram)
    strict = jnp.triu(gram, 1) / scales[:, None]
    identity = jnp.eye(width, dtype=gram.dtype)
    power = -strict
    total = identity + power
    for level in range((width - 1).bit_length() - 1):
        power = precise(power, power)
        total = precise(total, identity + power)
    return total / scales[None, :]


def expand_panel(panel, tile_map, ritz_basis):
    tile_count = tile_map.shape[0]
    tiles = panel.reshape(tile_count, TILE, panel.shape[1])
    places = jnp.arange(tile_count, dtype=jnp.int32)
    mover = (places[:, None] == tile_map[None, :]).astype(jnp.bfloat16)
    ordered = jnp.einsum("gs,sip->gip", mover, tiles, preferred_element_type=jnp.float32)
    ordered = ordered.astype(jnp.bfloat16).reshape(panel.shape[0], panel.shape[1])
    return jnp.dot(ritz_basis, ordered, preferred_element_type=jnp.float32)


def per_device(eigvecs, house_one, house_two, tile_map, select, ritz_basis):
    vec_one, vec_two = (
        lax.all_gather(house_one, "col", axis=1, tiled=True),
        lax.all_gather(house_two, "col", axis=1, tiled=True),
    )

    def apply_block(field, vectors):
        projected, gram = lax.psum((precise(vectors.T, field), precise(vectors.T, vectors)), "row")
        return field - precise(vectors, precise(compact(gram), projected))

    section = apply_block(eigvecs, vec_two)
    back_vectors = apply_block(section, vec_one)
    local_cols = eigvecs.shape[1]
    col_ids = lax.axis_index("col") * local_cols + jnp.arange(local_cols, dtype=jnp.int32)
    chooser = (col_ids[:, None] == select[None, :]).astype(jnp.float32)
    picked = precise(back_vectors, chooser)
    rows_part = lax.psum(picked.astype(jnp.bfloat16), "col")
    panel = lax.all_gather(rows_part, "row", axis=0, tiled=True)
    modes = expand_panel(panel, tile_map, ritz_basis)
    return (back_vectors, modes.astype(jnp.bfloat16))


def solution(mesh):
    return jax.shard_map(
        per_device,
        mesh=mesh,
        in_specs=(
            P("row", "col"),
            P("row", "col"),
            P("row", "col"),
            P(),
            P(),
            P(("row", "col"), None),
        ),
        out_specs=(P("row", "col"), P(("row", "col"), None)),
        check_vma=False,
    )
```

profile of v0, /device:TPU:0, one launch (start us, length us, event | category | flops | bytes accessed | tf_op | source)
XLA Modules:
  0.0 253.1 jit_solution(4916615402586915821)
XLA Ops:
  7.2 16.8 %all_gather.9 = f32[1024,128]{0,1:T(8,128)S(1)} all-gather(f32[1024,16]{0,1:T(8,128)} %param.8), channel_id=1, replica_groups=mesh['row'=4,'col'=8] {'col'}, dimensions={1}, use_global_device_ids=true | all-gather | bytes 589824 | tf_op jit(solution)/shard_map/all_gather | solution.py:39
  24.0 1.2 fusion.24
  25.2 3.6 %fusion.29 = f32[128,512]{1,0:T(8,128)} fusion(f32[1024,128]{0,1:T(8,128)S(1)} %all_gather.9, f32[1024,512]{1,0:T(8,128)} %param.6), kind=kOutput, calls=%fused_computation.58 | convolution fusion | flops 805306368 | bytes 2883584 | tf_op jit(solution)/shard_map/dot_general | solution.py:10
  28.9 1.8 copy.12
  30.7 14.7 %all_gather.10 = f32[1024,128]{0,1:T(8,128)S(1)} all-gather(f32[1024,16]{0,1:T(8,128)S(1)} %copy-done.4), channel_id=1, replica_groups=mesh['row'=4,'col'=8] {'col'}, dimensions={1}, use_global_device_ids=true | all-gather | bytes 589824 | tf_op jit(solution)/shard_map/all_gather | solution.py:38
  45.4 1.2 fusion.31
  46.7 27.0 %all-reduce.10.cloned.1.call-done = (f32[128,128]{1,0:T(8,128)}, f32[128,512]{1,0:T(8,128)}) async-done(((f32[128,128]{1,0:T(8,128)}, f32[128,512]{1,0:T(8,128)}), (f32[128,128]{1,0:T(8,128)}, f32[128,512]{1,0:T(8,128)})) %all-reduce.10.cloned.1.call-update) | async-done | bytes 327696 | tf_op jit(solution)/shard_map/psum | solution.py:43
  73.7 2.0 gather_fusion
  75.7 1.2 fusion.22
  76.9 1.1 fusion.9
  78.0 0.2 fusion.25
  78.2 0.2 fusion.26
  78.4 0.2 fusion.10
  78.6 0.2 fusion.27
  78.8 0.2 fusion.11
  79.1 0.2 fusion.28
  79.3 0.2 fusion.12
  79.5 0.2 convolution_add_fusion.1
  79.7 0.2 fusion.13
  79.9 0.2 convolution_divide_fusion.1
  80.1 0.4 fusion.30
  80.5 3.5 %bitcast_subtract_fusion.1 = f32[1024,512]{0,1:T(8,128)S(1)} fusion(f32[1024,512]{0,1:T(8,128)} %copy.12, f32[128,512]{1,0:T(8,128)S(1)} %fusion.30, f32[1024,128]{0,1:T(8,128)S(1)} %all_gather.9), kind=kOutput, calls=%fused_computation.3 | convolution fusion | flops 805830656 | bytes 4980736 | tf_op jit(solution)/shard_map/dot_general | solution.py:10
  84.0 2.5 convolution_bitcast_fusion
  86.5 0.2 all-reduce.6.cloned.1.call-start
  86.8 43.6 %all-reduce.8.cloned.1.call-done = (f32[128,128]{1,0:T(8,128)}, f32[128,512]{0,1:T(8,128)}) async-done(((f32[128,128]{1,0:T(8,128)}, f32[128,512]{0,1:T(8,128)}), (f32[128,128]{1,0:T(8,128)}, f32[128,512]{0,1:T(8,128)})) %all-reduce.8.cloned.1.call-update) | async-done | bytes 327696 | tf_op jit(solution)/shard_map/psum | solution.py:43
  130.3 2.0 gather_fusion.1
  132.3 1.2 fusion.23
  133.5 1.1 fusion.14
  134.6 0.2 fusion.32
  134.8 0.2 fusion.33
  135.1 0.2 fusion.15
  135.3 0.2 fusion.34
  135.5 0.2 fusion.16
  135.9 0.2 fusion.17
  136.1 0.2 convolution_add_fusion
  136.3 0.2 fusion.18
  136.6 0.2 convolution_divide_fusion
  136.8 0.4 fusion.36
  137.2 1.9 bitcast_subtract_fusion
  139.1 1.3 copy-done
  140.4 2.7 %convolution_convert_fusion.1 = bf16[1024,256]{1,0:T(8,128)(2,1)} fusion(f32[1024,512]{0,1:T(8,128)S(1)} %bitcast_subtract_fusion, s32[256]{0:T(256)S(1)} %copy-done.5, s32[512]{0:T(512)S(1)} %iota_add_fusion), kind=kOutput, calls=%fused_computation.8 | convolution fusion | flops 1611005952 | bytes 2624512 | tf_op jit(solution)/shard_map/dot_general | solution.py:10
  143.2 56.2 %all-reduce.6.cloned.1.call-done = bf16[1024,256]{1,0:T(8,128)(2,1)} async-done(((bf16[1024,256]{1,0:T(8,128)(2,1)}), bf16[1024,256]{1,0:T(8,128)(2,1)}) %all-reduce.6.cloned.1.call-update) | async-done | bytes 524304 | tf_op jit(solution)/shard_map/psum | solution.py:52
  199.5 2.9 %copy.15 = f32[1024,512]{1,0:T(8,128)} copy(f32[1024,512]{0,1:T(8,128)} %copy-done) | data formatting | bytes 4194304
  202.4 33.2 %all-gather.2.cloned.1.call-done = bf16[4096,256]{1,0:T(8,128)(2,1)} async-done(((bf16[1024,256]{1,0:T(8,128)(2,1)}), bf16[4096,256]{1,0:T(8,128)(2,1)}) %all-gather.2.cloned.1.call-update) | async-done | bytes 2097168 | tf_op jit(solution)/shard_map/all_gather | solution.py:53
  235.6 3.0 %fusion.2 = bf16[32,128,256]{2,0,1:T(8,128)(2,1)S(1)} fusion(bf16[32,128,256]{2,1,0:T(8,128)(2,1)} %bitcast.66, s32[32]{0:T(128)S(1)} %copy-done.6), kind=kOutput, calls=%fused_computation.6 | convolution fusion | flops 68158464 | bytes 4194432 | tf_op jit(solution)/shard_map/gs,sip->gip/dot_general | solution.py:31
  238.6 1.2 copy.14
  239.7 5.8 %fusion.5 = bf16[1024,256]{0,1:T(8,128)(2,1)S(1)} fusion(bf16[4096,256]{1,0:T(8,128)(2,1)S(1)} %bitcast.67, bf16[1024,4096]{1,0:T(8,128)(2,1)} %param.11), kind=kOutput, calls=%fused_computation.9 | convolution fusion | flops 2147745792 | bytes 11010048 | tf_op jit(solution)/shard_map/dot_general | solution.py:33
  245.5 1.0 copy.16
  (25 shorter events, 0.4 us)
Async XLA Ops:
  7.2 66.5 %all-reduce.10.cloned.1.call-start = ((), (), s32[]{:S(2)}) async-start(), calls=%async_computation.3 | async-start | bytes 655360 | tf_op jit(solution)/shard_map/psum | solution.py:43
  24.0 4.9 %copy-start.1 = (f32[1024,512]{1,0:T(8,128)S(1)}, f32[1024,512]{1,0:T(8,128)}, u32[]{:S(2)}) copy-start(f32[1024,512]{1,0:T(8,128)} %param.6) | copy-start | bytes 6291460
  28.8 1.9 copy-start.4
  28.8 101.5 %all-reduce.8.cloned.1.call-start = ((), (), s32[]{:S(2)}) async-start(), calls=%async_computation.2 | async-start | bytes 655360 | tf_op jit(solution)/shard_map/psum | solution.py:43
  73.7 6.4 %copy-start.3 = (f32[128,512]{1,0:T(8,128)S(1)}, f32[128,512]{1,0:T(8,128)}, u32[]{:S(2)}) copy-start(f32[128,512]{1,0:T(8,128)} %get-tuple-element.9) | copy-start | bytes 786436
  86.5 112.9 %all-reduce.6.cloned.1.call-start = ((), (), s32[]{:S(2)}) async-start(), calls=%async_computation | async-start | bytes 1048576 | tf_op jit(solution)/shard_map/psum | solution.py:52
  130.3 6.4 %copy-start.2 = (f32[128,512]{0,1:T(8,128)S(1)}, f32[128,512]{0,1:T(8,128)}, u32[]{:S(2)}) copy-start(f32[128,512]{0,1:T(8,128)} %get-tuple-element.7) | copy-start | bytes 786436
  137.2 3.2 %copy-start.5 = (s32[256]{0:T(256)S(1)}, s32[256]{0:T(256)}, u32[]{:S(2)}) copy-start(s32[256]{0:T(256)} %param.10) | copy-start | bytes 3076
  139.1 1.3 copy-start
  143.1 92.5 %all-gather.2.cloned.1.call-start = ((), (), s32[]{:S(2)}) async-start(), calls=%async_computation.1 | async-start | bytes 2621440 | tf_op jit(solution)/shard_map/all_gather | solution.py:53
  199.5 36.1 %copy-start.6 = (s32[32]{0:T(128)S(1)}, s32[32]{0:T(128)}, u32[]{:S(2)}) copy-start(s32[32]{0:T(128)} %param.9) | copy-start | bytes 388
Sparse Core Ops, SparseCore 0:
  29.0 44.6 all-reduce.9
  86.7 43.6 all-reduce.7
  143.3 56.1 all-reduce.5
  201.3 34.2 all-gather.1
where the time goes:
time: 254 us; the launch traced here: 253 us
  waiting for transfers between devices  160 us (63%)
  matrix products  34.8 us (14%)
  blocking collectives  31.5 us (12%)
  between operations  14.1 us (6%)
  local copies, waits for them, and re-layouts  12.2 us (5%)
    psum x2, waiting for transfers between devices, apply_block(): lax.psum((precise(vectors.T, field), precise(vectors.T, vectors)), 'row')  70.6 us
    psum x1, waiting for transfers between devices, per_device(): rows_part = lax.psum(picked.astype(jnp.bfloat16), 'col')  56.2 us
    all_gather x1, waiting for transfers between devices, per_device(): panel = lax.all_gather(rows_part, 'row', axis=0, tiled=True)  33.2 us
    dot_general x33, matrix products, precise(): jnp.dot(left, right, precision=lax.Precision.HIGHEST, preferred_element_t...  26.1 us
    all_gather x1, blocking collectives, per_device(): lax.all_gather(house_two, 'col', axis=1, tiled=True)  16.8 us
    all_gather x1, blocking collectives, per_device(): lax.all_gather(house_one, 'col', axis=1, tiled=True)  14.7 us
    unnamed x17, local copies, waits for them, and re-layouts  7.04 us
    dot_general x1, matrix products, expand_panel(): return jnp.dot(ritz_basis, ordered, preferred_element_type=jnp.float32)  5.77 us
  transfers between devices with their start and end apart: 4, of which 4 were waited for; matrix products, arithmetic and copies ran while one was open for 2% of the time, Pallas kernels for 0%

commit v1 on v0

--- a/solution.py
+++ b/solution.py
@@ -49,7 +49,7 @@
     col_ids = lax.axis_index("col") * local_cols + jnp.arange(local_cols, dtype=jnp.int32)
     chooser = (col_ids[:, None] == select[None, :]).astype(jnp.float32)
     picked = precise(back_vectors, chooser)
-    rows_part = lax.psum(picked.astype(jnp.bfloat16), "col")
+    rows_part = jnp.sum(lax.all_gather(picked.astype(jnp.bfloat16), "col"), axis=0)
     panel = lax.all_gather(rows_part, "row", axis=0, tiled=True)
     modes = expand_panel(panel, tile_map, ritz_basis)
     return (back_vectors, modes.astype(jnp.bfloat16))

time: 254 us -> 246 us (0.969)
  waiting for transfers between devices: 160 us -> 150 us
  other arithmetic: 0.02 us -> 3.86 us
    psum x1 -> x0, waiting for transfers between devices: 56.2 us -> none  [per_device(): rows_part = lax.psum(picked.astype(jnp.bfloat16), 'col')]
    all_gather x0 -> x1, waiting for transfers between devices: none -> 47 us  [per_device(): lax.all_gather(picked.astype(jnp.bfloat16), 'col')]
    reduce_sum x0 -> x1, other arithmetic: none -> 3.83 us  [per_device(): jnp.sum(lax.all_gather(picked.astype(jnp.bfloat16), 'col'), axis=0)]
    unnamed x17 -> x19, local copies, waits for them, and re-layouts: 7.04 us -> 5.98 us
where the time goes in v1:
time: 246 us
  waiting for transfers between devices  150 us (61%)
  matrix products  34.8 us (14%)
  blocking collectives  31.5 us (13%)
  between operations  14.1 us (6%)
  local copies, waits for them, and re-layouts  11.1 us (5%)
  other arithmetic  3.86 us (2%)
    psum x2, waiting for transfers between devices, apply_block(): lax.psum((precise(vectors.T, field), precise(vectors.T, vectors)), 'row')  70.6 us
    all_gather x1, waiting for transfers between devices, per_device(): lax.all_gather(picked.astype(jnp.bfloat16), 'col')  47 us
    all_gather x1, waiting for transfers between devices, per_device(): panel = lax.all_gather(rows_part, 'row', axis=0, tiled=True)  32.3 us
    dot_general x33, matrix products, precise(): jnp.dot(left, right, precision=lax.Precision.HIGHEST, preferred_element_t...  26 us
    all_gather x1, blocking collectives, per_device(): lax.all_gather(house_two, 'col', axis=1, tiled=True)  16.8 us
    all_gather x1, blocking collectives, per_device(): lax.all_gather(house_one, 'col', axis=1, tiled=True)  14.7 us
    unnamed x19, local copies, waits for them, and re-layouts  5.98 us
    dot_general x1, matrix products, expand_panel(): return jnp.dot(ritz_basis, ordered, preferred_element_type=jnp.float32)  5.77 us
  transfers between devices with their start and end apart: 4, of which 4 were waited for; matrix products, arithmetic and copies ran while one was open for 2% of the time, Pallas kernels for 0%

profile of v1, /device:TPU:0, one launch (start us, length us, event | category | flops | bytes accessed | tf_op | source)
XLA Modules:
  0.0 245.9 jit_solution(17700642528129598380)
XLA Ops:
  7.2 16.8 %all_gather.15 = f32[1024,128]{0,1:T(8,128)S(1)} all-gather(f32[1024,16]{0,1:T(8,128)} %param.8), channel_id=1, replica_groups=mesh['row'=4,'col'=8] {'col'}, dimensions={1}, use_global_device_ids=true | all-gather | bytes 589824 | tf_op jit(solution)/shard_map/all_gather | solution.py:39
  24.0 1.2 fusion.24
  25.2 3.6 %fusion.29 = f32[128,512]{1,0:T(8,128)} fusion(f32[1024,128]{0,1:T(8,128)S(1)} %all_gather.15, f32[1024,512]{1,0:T(8,128)} %param.6), kind=kOutput, calls=%fused_computation.58 | convolution fusion | flops 805306368 | bytes 2883584 | tf_op jit(solution)/shard_map/dot_general | solution.py:10
  28.9 1.8 copy.11
  30.7 14.7 %all_gather.16 = f32[1024,128]{0,1:T(8,128)S(1)} all-gather(f32[1024,16]{0,1:T(8,128)S(1)} %copy-done.5), channel_id=1, replica_groups=mesh['row'=4,'col'=8] {'col'}, dimensions={1}, use_global_device_ids=true | all-gather | bytes 589824 | tf_op jit(solution)/shard_map/all_gather | solution.py:38
  45.4 1.2 fusion.31
  46.6 27.0 %all-reduce.7.cloned.1.call-done = (f32[128,128]{1,0:T(8,128)}, f32[128,512]{1,0:T(8,128)}) async-done(((f32[128,128]{1,0:T(8,128)}, f32[128,512]{1,0:T(8,128)}), (f32[128,128]{1,0:T(8,128)}, f32[128,512]{1,0:T(8,128)})) %all-reduce.7.cloned.1.call-update) | async-done | bytes 327696 | tf_op jit(solution)/shard_map/psum | solution.py:43
  73.7 2.0 gather_fusion
  75.7 1.2 fusion.22
  76.9 1.1 fusion.9
  78.0 0.2 fusion.25
  78.2 0.2 fusion.26
  78.4 0.2 fusion.10
  78.8 0.2 fusion.11
  79.0 0.2 fusion.28
  79.3 0.2 fusion.12
  79.5 0.2 convolution_add_fusion.1
  79.7 0.2 fusion.13
  79.9 0.2 convolution_divide_fusion.1
  80.1 0.4 fusion.30
  80.5 3.5 %bitcast_subtract_fusion.1 = f32[1024,512]{0,1:T(8,128)S(1)} fusion(f32[1024,512]{0,1:T(8,128)} %copy.11, f32[128,512]{1,0:T(8,128)S(1)} %fusion.30, f32[1024,128]{0,1:T(8,128)S(1)} %all_gather.15), kind=kOutput, calls=%fused_computation.3 | convolution fusion | flops 805830656 | bytes 4980736 | tf_op jit(solution)/shard_map/dot_general | solution.py:10
  84.0 2.5 %convolution_bitcast_fusion = f32[128,512]{0,1:T(8,128)} fusion(f32[1024,512]{0,1:T(8,128)S(1)} %bitcast_subtract_fusion.1, f32[1024,128]{0,1:T(8,128)S(1)} %all_gather.16), kind=kOutput, calls=%fused_computation.10 | convolution fusion | flops 805306368 | bytes 2883584 | tf_op jit(solution)/shard_map/dot_general | solution.py:10
  86.5 0.2 all-gather.6.cloned.1.call-start
  86.8 43.6 %all-reduce.5.cloned.1.call-done = (f32[128,128]{1,0:T(8,128)}, f32[128,512]{0,1:T(8,128)}) async-done(((f32[128,128]{1,0:T(8,128)}, f32[128,512]{0,1:T(8,128)}), (f32[128,128]{1,0:T(8,128)}, f32[128,512]{0,1:T(8,128)})) %all-reduce.5.cloned.1.call-update) | async-done | bytes 327696 | tf_op jit(solution)/shard_map/psum | solution.py:43
  130.3 2.0 gather_fusion.1
  132.3 1.2 fusion.23
  133.5 1.1 fusion.14
  134.8 0.2 fusion.33
  135.1 0.2 fusion.15
  135.3 0.2 fusion.34
  135.5 0.2 fusion.16
  135.9 0.2 fusion.17
  136.1 0.2 convolution_add_fusion
  136.3 0.2 fusion.18
  136.5 0.2 convolution_divide_fusion
  136.8 0.4 fusion.36
  137.2 1.9 bitcast_subtract_fusion
  139.1 1.3 copy-done
  140.4 2.7 %convolution_convert_fusion.1 = bf16[1024,256]{1,0:T(8,128)(2,1)} fusion(f32[1024,512]{0,1:T(8,128)S(1)} %bitcast_subtract_fusion, s32[256]{0:T(256)S(1)} %copy-done.6, s32[512]{0:T(512)S(1)} %iota_add_fusion), kind=kOutput, calls=%fused_computation.8 | convolution fusion | flops 1611005952 | bytes 2624512 | tf_op jit(solution)/shard_map/dot_general | solution.py:10
  143.1 0.3 all-gather.4.cloned.1.call-start
  143.4 47.0 %all-gather.6.cloned.1.call-done = bf16[8192,256]{1,0:T(8,128)(2,1)} async-done(((bf16[1024,256]{1,0:T(8,128)(2,1)}), bf16[8192,256]{1,0:T(8,128)(2,1)}) %all-gather.6.cloned.1.call-update) | async-done | bytes 4194320 | tf_op jit(solution)/shard_map/all_gather | solution.py:52
  190.4 3.8 %reduce_sum.12 = bf16[1024,256]{1,0:T(8,128)(2,1)} reduce(bf16[8,1024,256]{2,1,0:T(8,128)(2,1)} %bitcast.67, bf16[]{:T(256)} %constant.23.clone.1), dimensions={0}, to_apply=%region_4.5 | reduce | flops 1835008 | bytes 4718594 | tf_op jit(solution)/shard_map/reduce_sum | solution.py:52
  194.3 1.8 copy.14
  196.1 32.3 %all-gather.4.cloned.1.call-done = bf16[4096,256]{1,0:T(8,128)(2,1)} async-done(((bf16[1024,256]{1,0:T(8,128)(2,1)}), bf16[4096,256]{1,0:T(8,128)(2,1)}) %all-gather.4.cloned.1.call-update) | async-done | bytes 2097168 | tf_op jit(solution)/shard_map/all_gather | solution.py:53
  228.5 3.0 %fusion.2 = bf16[32,128,256]{2,0,1:T(8,128)(2,1)S(1)} fusion(bf16[32,128,256]{2,1,0:T(8,128)(2,1)} %bitcast.68, s32[32]{0:T(128)S(1)} %copy-done.7), kind=kOutput, calls=%fused_computation.6 | convolution fusion | flops 68158464 | bytes 4194432 | tf_op jit(solution)/shard_map/gs,sip->gip/dot_general | solution.py:31
  231.4 1.2 copy.13
  232.6 5.8 %fusion.5 = bf16[1024,256]{0,1:T(8,128)(2,1)S(1)} fusion(bf16[4096,256]{1,0:T(8,128)(2,1)S(1)} %bitcast.69, bf16[1024,4096]{1,0:T(8,128)(2,1)} %param.11), kind=kOutput, calls=%fused_computation.9 | convolution fusion | flops 2147745792 | bytes 11010048 | tf_op jit(solution)/shard_map/dot_general | solution.py:33
  238.4 1.0 copy.15
  (28 shorter events, 0.8 us)
Async XLA Ops:
  7.2 66.5 %all-reduce.7.cloned.1.call-start = ((), (), s32[]{:S(2)}) async-start(), calls=%async_computation.3 | async-start | bytes 655360 | tf_op jit(solution)/shard_map/psum | solution.py:43
  24.0 4.9 %copy-start.2 = (f32[1024,512]{1,0:T(8,128)S(1)}, f32[1024,512]{1,0:T(8,128)}, u32[]{:S(2)}) copy-start(f32[1024,512]{1,0:T(8,128)} %param.6) | copy-start | bytes 6291460
  28.8 1.9 copy-start.5
  28.8 101.5 %all-reduce.5.cloned.1.call-start = ((), (), s32[]{:S(2)}) async-start(), calls=%async_computation.2 | async-start | bytes 655360 | tf_op jit(solution)/shard_map/psum | solution.py:43
  73.7 6.4 %copy-start.4 = (f32[128,512]{1,0:T(8,128)S(1)}, f32[128,512]{1,0:T(8,128)}, u32[]{:S(2)}) copy-start(f32[128,512]{1,0:T(8,128)} %get-tuple-element.9) | copy-start | bytes 786436
  86.5 103.9 %all-gather.6.cloned.1.call-start = ((), (), s32[]{:S(2)}) async-start(), calls=%async_computation.1 | async-start | bytes 4718592 | tf_op jit(solution)/shard_map/all_gather | solution.py:52
  130.3 6.4 %copy-start.3 = (f32[128,512]{0,1:T(8,128)S(1)}, f32[128,512]{0,1:T(8,128)}, u32[]{:S(2)}) copy-start(f32[128,512]{0,1:T(8,128)} %get-tuple-element.7) | copy-start | bytes 786436
  137.1 3.2 %copy-start.6 = (s32[256]{0:T(256)S(1)}, s32[256]{0:T(256)}, u32[]{:S(2)}) copy-start(s32[256]{0:T(256)} %param.10) | copy-start | bytes 3076
  139.1 1.3 copy-start
  143.1 85.3 %all-gather.4.cloned.1.call-start = ((), (), s32[]{:S(2)}) async-start(), calls=%async_computation | async-start | bytes 2621440 | tf_op jit(solution)/shard_map/all_gather | solution.py:53
  190.4 3.9 %copy-start.1 = (f32[1024,512]{0,1:T(8,128)S(1)}, f32[1024,512]{0,1:T(8,128)}, u32[]{:S(2)}) copy-start(f32[1024,512]{0,1:T(8,128)} %copy-done) | copy-start | bytes 6291460
  194.3 34.2 %copy-start.7 = (s32[32]{0:T(128)S(1)}, s32[32]{0:T(128)}, u32[]{:S(2)}) copy-start(s32[32]{0:T(128)} %param.9) | copy-start | bytes 388
Sparse Core Ops, SparseCore 0:
  28.9 44.6 all-reduce.6
  86.6 43.6 all-reduce.4
  143.3 47.1 all-gather.5
  194.4 34.0 all-gather.3
